TPU v7x, 32 devices: a whole 2x2x4 slice. The times are simulated.
32 devices in a mesh: ctx: 8 (over z, y), grp: 4 (over x, core).
Axes of the slice: x: 2, y: 2, z: 4, core: 2. Of those that a mesh axis runs over, the one named last changes fastest.
Arguments:
- streams: bfloat16 [3, 3072, 4096], P(None, 'ctx', 'grp'), may hold values from -400 to 400
- filters: bfloat16 [3, 256, 128], P(None, 'grp'), may hold values from -0.5 to 0.5
- gain: float32 [4096], P('grp'), may hold values from 0.5 to 1.5
Outputs:
- normed: bfloat16 [3072, 4096], P('ctx', 'grp')
All inputs are finite; a program needn't handle non-finite values.
Results may differ from a plain program's by a relative error of at most 0.012.
The roundings to bfloat16 on the way count: a program that leaves them out, or rounds other values in their place, can miss the bound.
Values may be sent and summed in bfloat16 or wider, within the bound.
A program may use at most 128 MiB of HBM per device.

v0:
```python
import math

import jax
import jax.numpy as jnp
import numpy as np
from jax import lax
from jax.sharding import PartitionSpec as P

HD = 128
CH = 4096


def passed_along(block, axis, distance):
    devices = range(lax.axis_size(axis))
    route = [(i - distance, i) for i in devices if i - distance in devices]
    return lax.ppermute(block, axis, route)


def filter_all(streams, filters):
    tok_rows = streams.shape[1]
    chan_count = streams.shape[2]
    filt_len = filters.shape[2]
    group_count = filters.shape[1]
    group_width = chan_count // group_count
    tail = streams[:, tok_rows - filt_len :, :]
    before = passed_along(tail, "ctx", 1)
    padded = jnp.concatenate([before, streams], axis=1)
    block_count = tok_rows // filt_len
    blocks = padded.reshape(3, block_count + 1, filt_len, group_count, group_width)
    lag_table = np.arange(filt_len)[:, None] - np.arange(filt_len)[None, :]
    lower_idx = np.where(lag_table >= 0, lag_table, 0)
    upper_idx = np.where(lag_table < 0, lag_table + filt_len, 0)
    lower = jnp.where(lag_table >= 0, filters[:, :, lower_idx], 0.0)
    upper = jnp.where(lag_table < 0, filters[:, :, upper_idx], 0.0)
    result = jnp.einsum(
        "agts,absgc->abtgc", lower, blocks[:, 1:], preferred_element_type=jnp.float32
    )
    result = result + jnp.einsum(
        "agts,absgc->abtgc", upper, blocks[:, :-1], preferred_element_type=jnp.float32
    )
    return result.reshape(3, tok_rows, chan_count).astype(jnp.bfloat16)


def attend(queries, positions, keyed, valued):
    tok_rows, chan_count = queries.shape
    head_count = chan_count // HD
    scale = HD ** (-0.5)
    query_heads = queries.reshape(tok_rows, head_count, HD)
    query_last = jnp.max(positions)
    start_state = (
        jnp.full((head_count, tok_rows), -1e30, jnp.float32),
        jnp.zeros((head_count, tok_rows), jnp.float32),
        jnp.zeros((tok_rows, head_count, HD), jnp.float32),
    )
    key_piece = lax.all_gather(keyed, "ctx", axis=0, tiled=True)
    value_piece = lax.all_gather(valued, "ctx", axis=0, tiled=True)
    piece_len = key_piece.shape[0]
    block_len = math.gcd(piece_len, 512)

    def step_block(step_idx, state):
        offset = step_idx * block_len
        key_block = lax.dynamic_slice_in_dim(key_piece, offset, block_len, 0).reshape(
            block_len, head_count, HD
        )
        value_block = lax.dynamic_slice_in_dim(value_piece, offset, block_len, 0).reshape(
            block_len, head_count, HD
        )
        key_pos = offset + jnp.arange(block_len, dtype=jnp.int32)

        def update_block(inner):
            running, totals, accum = inner
            scores = (
                jnp.einsum(
                    "shd,khd->hsk", query_heads, key_block, preferred_element_type=jnp.float32
                )
                * scale
            )
            causal = key_pos[None, None, :] <= positions[None, :, None]
            newtop = jnp.maximum(running, jnp.max(jnp.where(causal, scores, -1e30), axis=2))
            weights = jnp.where(causal, jnp.exp(scores - newtop[:, :, None]), 0.0)
            factor = jnp.exp(running - newtop)
            totals = totals * factor + jnp.sum(weights, axis=2)
            accum = accum * factor.T[:, :, None] + jnp.einsum(
                "hsk,khd->shd",
                weights.astype(jnp.bfloat16),
                value_block,
                preferred_element_type=jnp.float32,
            )
            return (newtop, totals, accum)

        return lax.cond(offset > query_last, lambda inner: inner, update_block, state)

    running, totals, accum = lax.fori_loop(0, piece_len // block_len, step_block, start_state)
    return (accum / totals.T[:, :, None]).reshape(tok_rows, chan_count).astype(jnp.bfloat16)


def local(streams, filters, gain):
    features = filter_all(streams, filters)
    tok_rows = streams.shape[1]
    my_index = lax.axis_index("ctx")
    queries = features[0]
    positions = my_index * tok_rows + jnp.arange(tok_rows, dtype=jnp.int32)
    attended = attend(queries, positions, features[1], features[2])
    wide = attended.astype(jnp.float32)
    power = lax.psum(jnp.sum(wide * wide, axis=1), "grp") / CH
    return (wide * gain[None, :] * lax.rsqrt(power + 1e-06)[:, None]).astype(jnp.bfloat16)


def solution(mesh):
    placed = (P(None, "ctx", "grp"), P(None, "grp", None), P("grp"))
    return jax.shard_map(
        local, mesh=mesh, in_specs=placed, out_specs=P("ctx", "grp"), check_vma=False
    )
```

profile of v0, /device:TPU:29, one launch (start us, length us, event | category | flops | bytes accessed | tf_op | source)
XLA Modules:
  0.0 566.1 jit_solution(7154377040794997620)
XLA Ops:
  10.8 112.9 %gather_fusion.1 = bf16[16384,3,64]{2,1,0:T(4,128)(2,1)} fusion(bf16[3,64,128]{1,0,2:T(4,128)(2,1)S(1)} %copy.17, s32[16384]{0:T(1024)S(1)} %broadcast_clamp_fusion), kind=kCustom, calls=%fused_computation.1 | custom fusion | bytes 12648448 | tf_op jit(solution)/shard_map/gather | solution.py:34
  123.7 17.2 %copy.21 = bf16[128,128,3,64]{1,0,3,2:T(8,128)(2,1)} copy(bf16[128,128,3,64]{3,2,1,0:T(4,128)(2,1)} %bitcast.81) | data formatting | bytes 12582912 | tf_op jit(solution)/shard_map/gather | solution.py:34
  141.0 112.7 %gather_fusion = bf16[16384,3,64]{2,1,0:T(4,128)(2,1)} fusion(bf16[3,64,128]{1,0,2:T(4,128)(2,1)S(1)} %copy.17, s32[16384]{0:T(1024)S(1)} %broadcast_clamp_fusion.1), kind=kCustom, calls=%fused_computation | custom fusion | bytes 12648448 | tf_op jit(solution)/shard_map/gather | solution.py:33
  253.8 17.2 %copy.18 = bf16[128,128,3,64]{1,0,3,2:T(8,128)(2,1)} copy(bf16[128,128,3,64]{3,2,1,0:T(4,128)(2,1)} %bitcast.80) | data formatting | bytes 12582912 | tf_op jit(solution)/shard_map/gather | solution.py:33
  273.1 3.0 copy.15
  276.1 5.7 %reshape.74 = bf16[3,4,128,64,16]{2,1,4,3,0:T(4,128)(2,1)} reshape(bf16[3,512,1024]{1,2,0:T(8,128)(2,1)} %copy.15) | data formatting | bytes 6291456 | tf_op jit(solution)/shard_map/reshape | solution.py:29
  281.8 8.0 %fusion.40 = (bf16[3,3,128,64,16]{2,1,4,3,0:T(4,128)(2,1)}, bf16[3,3,128,64,16]{2,1,4,3,0:T(4,128)(2,1)S(1)}) fusion(bf16[3,4,128,64,16]{2,1,4,3,0:T(4,128)(2,1)} %reshape.74), kind=kLoop, calls=%fused_computation.56 | loop fusion | bytes 9437184 | tf_op jit(solution)/shard_map/slice | solution.py:36
  289.9 6.0 %fusion.18 = f32[3,64,3,16,128]{4,3,2,1,0:T(8,128)} fusion(bf16[128,128,3,64]{1,0,3,2:T(8,128)(2,1)S(1)} %bitcast.79, pred[128,128]{1,0:T(8,128)(4,1)S(1)} %bitcast.89, bf16[3,3,128,64,16]{2,1,4,3,0:T(4,128)(2,1)S(1)} %get-tuple-element.351), kind=kOutput, calls=%fused_computation.26 | convolution fusion | flops 305135616 | bytes 13385728 | tf_op jit(solution)/shard_map/agts,absgc->abtgc/dot_general | solution.py:38
  295.9 7.8 %fusion.28 = bf16[3,3,128,64,16]{2,4,1,3,0:T(8,128)(2,1)S(1)} fusion(f32[3,64,3,16,128]{4,3,2,1,0:T(8,128)} %fusion.18, bf16[128,128,3,64]{1,0,3,2:T(8,128)(2,1)S(1)} %bitcast.77, pred[128,128]{1,0:T(8,128)(4,1)S(1)} %bitcast.88, bf16[3,3,128,64,16]{2,1,4,3,0:T(4,128)(2,1)} %get-tuple-element.350), kind=kOutput, calls=%fused_computation.38 | convolution fusion | flops 307494912 | bytes 15745024 | tf_op jit(solution)/shard_map/agts,absgc->abtgc/dot_general | solution.py:35
  309.9 94.8 %all-gather.3.cloned.1.call-done = bf16[3072,1024]{0,1:T(8,128)(2,1)} async-done(((bf16[384,1024]{0,1:T(8,128)(2,1)}), bf16[3072,1024]{0,1:T(8,128)(2,1)}) %all-gather.3.cloned.1.call-update) | async-done | bytes 6291472 | tf_op jit(solution)/shard_map/all_gather | solution.py:55
  404.7 99.8 %all-gather.5.cloned.1.call-done = bf16[3072,1024]{0,1:T(8,128)(2,1)} async-done(((bf16[384,1024]{0,1:T(8,128)(2,1)}), bf16[3072,1024]{0,1:T(8,128)(2,1)}) %all-gather.5.cloned.1.call-update) | async-done | bytes 6291472 | tf_op jit(solution)/shard_map/all_gather | solution.py:56
  504.6 47.3 %while.18 = (s32[]{:T(128)}, f32[8,384]{1,0:T(8,128)S(1)}, f32[8,384]{1,0:T(8,128)S(1)}, f32[384,8,128]{2,0,1:T(8,128)S(1)}, s32[]{:T(128)}, /*index=5*/bf16[307...) while((s32[]{:T(128)}, f32[8,384]{1,0:T(8,128)S(1)}, ...), condition=%wide.region_6.7_spmd.clone, body=%wide.region_1.6_spmd.clone.sunk | while | flops 823601024 | bytes 30095668 | solution.py:93
  505.2 7.3 %conditional.3 = (f32[8,384]{1,0:T(8,128)S(1)}, f32[8,384]{1,0:T(8,128)S(1)}, f32[384,8,128]{2,0,1:T(8,128)S(1)}) conditional(s32[]{:T(128)} %convert_element_type.65, (s32[]{:T(128)}, s32[512]{0:T(512)S(1)}, s32[]{:T(128)}, bf16[3072,1024]{0,1:T(8,128)(2,1)}, bf16[384,8,128]{2,0,1:T(8,128)(2,1)S(1)}, /*index=5*/f32[8,384]{1,0:T(8,128)S(1)}, ...), branch_computations={%region_2.4_spmd, %region_5.5_spmd} | conditional | flops 823601024 | bytes 30067270 | solution.py:91
  508.7 2.5 bitcast_add_fusion
  513.1 7.3 %conditional.3 = (f32[8,384]{1,0:T(8,128)S(1)}, f32[8,384]{1,0:T(8,128)S(1)}, f32[384,8,128]{2,0,1:T(8,128)S(1)}) conditional(s32[]{:T(128)} %convert_element_type.65, (s32[]{:T(128)}, s32[512]{0:T(512)S(1)}, s32[]{:T(128)}, bf16[3072,1024]{0,1:T(8,128)(2,1)}, bf16[384,8,128]{2,0,1:T(8,128)(2,1)S(1)}, /*index=5*/f32[8,384]{1,0:T(8,128)S(1)}, ...), branch_computations={%region_2.4_spmd, %region_5.5_spmd} | conditional | flops 823601024 | bytes 30067270 | solution.py:91
  516.6 2.5 bitcast_add_fusion
  521.0 7.3 %conditional.3 = (f32[8,384]{1,0:T(8,128)S(1)}, f32[8,384]{1,0:T(8,128)S(1)}, f32[384,8,128]{2,0,1:T(8,128)S(1)}) conditional(s32[]{:T(128)} %convert_element_type.65, (s32[]{:T(128)}, s32[512]{0:T(512)S(1)}, s32[]{:T(128)}, bf16[3072,1024]{0,1:T(8,128)(2,1)}, bf16[384,8,128]{2,0,1:T(8,128)(2,1)S(1)}, /*index=5*/f32[8,384]{1,0:T(8,128)S(1)}, ...), branch_computations={%region_2.4_spmd, %region_5.5_spmd} | conditional | flops 823601024 | bytes 30067270 | solution.py:91
  524.4 2.5 bitcast_add_fusion
  528.9 7.3 %conditional.3 = (f32[8,384]{1,0:T(8,128)S(1)}, f32[8,384]{1,0:T(8,128)S(1)}, f32[384,8,128]{2,0,1:T(8,128)S(1)}) conditional(s32[]{:T(128)} %convert_element_type.65, (s32[]{:T(128)}, s32[512]{0:T(512)S(1)}, s32[]{:T(128)}, bf16[3072,1024]{0,1:T(8,128)(2,1)}, bf16[384,8,128]{2,0,1:T(8,128)(2,1)S(1)}, /*index=5*/f32[8,384]{1,0:T(8,128)S(1)}, ...), branch_computations={%region_2.4_spmd, %region_5.5_spmd} | conditional | flops 823601024 | bytes 30067270 | solution.py:91
  536.8 7.3 %conditional.3 = (f32[8,384]{1,0:T(8,128)S(1)}, f32[8,384]{1,0:T(8,128)S(1)}, f32[384,8,128]{2,0,1:T(8,128)S(1)}) conditional(s32[]{:T(128)} %convert_element_type.65, (s32[]{:T(128)}, s32[512]{0:T(512)S(1)}, s32[]{:T(128)}, bf16[3072,1024]{0,1:T(8,128)(2,1)}, bf16[384,8,128]{2,0,1:T(8,128)(2,1)S(1)}, /*index=5*/f32[8,384]{1,0:T(8,128)S(1)}, ...), branch_computations={%region_2.4_spmd, %region_5.5_spmd} | conditional | flops 823601024 | bytes 30067270 | solution.py:91
  540.2 2.5 bitcast_add_fusion
  544.7 7.3 %conditional.3 = (f32[8,384]{1,0:T(8,128)S(1)}, f32[8,384]{1,0:T(8,128)S(1)}, f32[384,8,128]{2,0,1:T(8,128)S(1)}) conditional(s32[]{:T(128)} %convert_element_type.65, (s32[]{:T(128)}, s32[512]{0:T(512)S(1)}, s32[]{:T(128)}, bf16[3072,1024]{0,1:T(8,128)(2,1)}, bf16[384,8,128]{2,0,1:T(8,128)(2,1)S(1)}, /*index=5*/f32[8,384]{1,0:T(8,128)S(1)}, ...), branch_computations={%region_2.4_spmd, %region_5.5_spmd} | conditional | flops 823601024 | bytes 30067270 | solution.py:91
  548.1 2.5 bitcast_add_fusion
  552.5 5.6 psum.7
  (111 shorter events, 45.0 us)
Async XLA Ops:
  6.5 398.2 %all-gather.3.cloned.1.call-start = ((), (), s32[]{:S(2)}) async-start(), calls=%async_computation | async-start | bytes 7077888 | tf_op jit(solution)/shard_map/all_gather | solution.py:55
  7.7 263.2 %collective-permute-start = (bf16[3,128,1024]{2,1,0:T(8,128)(2,1)S(1)}, bf16[3,128,1024]{2,1,0:T(8,128)(2,1)}, u32[]{:S(2)}, u32[]{:S(2)}) collective-permute-start(bf16[3,128,1024]{2,1,0:T(8,128)(2,1)S(1)} %slice.21), channel_id=1, source_target_pairs={{0,4},{4,8},{8,12},{12,16},{16,20},{20,24},{24,28},{1,5},{5,9},{9,... | collective-permute-start | bytes 2359304 | tf_op jit(solution)/shard_map/ppermute | solution.py:16
  123.7 17.3 %copy-start.2 = (s32[16384]{0:T(1024)S(1)}, s32[16384]{0:T(1024)}, u32[]{:S(2)}) copy-start(s32[16384]{0:T(1024)} %constant.103) | copy-start | bytes 196612
  276.1 13.7 %slice-start.2 = ((s8[6291456]{0:T(1024)(128)(4,1)}), s8[2097152]{0:T(1024)(128)(4,1)S(1)}, s32[]{:S(2)}) async-start(s8[6291456]{0:T(1024)(128)(4,1)} %bitcast.78), calls=%async_computation.4 | async-start | bytes 4194304
  281.8 8.1 %slice-start.3 = ((s8[6291456]{0:T(1024)(128)(4,1)}), s8[4194304]{0:T(1024)(128)(4,1)S(1)}, s32[]{:S(2)}) async-start(s8[6291456]{0:T(1024)(128)(4,1)} %bitcast.78), calls=%async_computation.5 | async-start | bytes 8388608
  281.8 8.1 %copy-start.1 = (pred[128,128]{1,0:T(32,128)(4,1)S(1)}, pred[128,128]{1,0:T(32,128)(4,1)}, u32[]{:S(2)}) copy-start(pred[128,128]{1,0:T(32,128)(4,1)} %constant.100.clone) | copy-start | bytes 49156
  281.8 14.1 %slice-start = ((s8[6291456]{0:T(1024)(128)(4,1)}), s8[4194304]{0:T(1024)(128)(4,1)S(1)}, s32[]{:S(2)}) async-start(s8[6291456]{0:T(1024)(128)(4,1)} %bitcast.76), calls=%async_computation.2 | async-start | bytes 8388608
  289.8 6.1 %slice-start.1 = ((s8[6291456]{0:T(1024)(128)(4,1)}), s8[2097152]{0:T(1024)(128)(4,1)S(1)}, s32[]{:S(2)}) async-start(s8[6291456]{0:T(1024)(128)(4,1)} %bitcast.76), calls=%async_computation.3 | async-start | bytes 4194304
  289.9 6.1 %copy-start = (pred[128,128]{1,0:T(32,128)(4,1)S(1)}, pred[128,128]{1,0:T(32,128)(4,1)}, u32[]{:S(2)}) copy-start(pred[128,128]{1,0:T(32,128)(4,1)} %constant.98.clone) | copy-start | bytes 49156
  305.7 198.7 %all-gather.5.cloned.1.call-start = ((), (), s32[]{:S(2)}) async-start(), calls=%async_computation.1 | async-start | bytes 7077888 | tf_op jit(solution)/shard_map/all_gather | solution.py:56
  504.6 53.5 %copy-start.3 = (f32[1024]{0:T(1024)S(1)}, f32[1024]{0:T(1024)}, u32[]{:S(2)}) copy-start(f32[1024]{0:T(1024)} %param.15) | copy-start | bytes 12292
Sparse Core Ops, SparseCore 0:
  305.9 98.8 all-gather.2
  406.8 97.6 all-gather.4
where the time goes:
time: 570 us; the launch traced here: 566 us
  local copies, waits for them, and re-layouts  294 us (52%)
  waiting for transfers between devices  195 us (34%)
  matrix products  37.7 us (7%)
  other arithmetic  14.4 us (3%)
  between operations  13.6 us (2%)
    gather x2, local copies, waits for them, and re-layouts, filter_all(): upper = jnp.where(lag_table < 0, filters[:, :, upper_idx], 0.0)  130 us
    gather x2, local copies, waits for them, and re-layouts, filter_all(): lower = jnp.where(lag_table >= 0, filters[:, :, lower_idx], 0.0)  130 us
    all_gather x1, waiting for transfers between devices, attend(): value_piece = lax.all_gather(valued, 'ctx', axis=0, tiled=True)  99.8 us
    all_gather x1, waiting for transfers between devices, attend(): key_piece = lax.all_gather(keyed, 'ctx', axis=0, tiled=True)  94.8 us
    dot_general x6, matrix products, update_block(): jnp.einsum('hsk,khd->shd', weights.astype(jnp.bfloat16), value_block, pre...  14.9 us
  transfers between devices with their start and end apart: 3, of which 2 were waited for; matrix products, arithmetic and copies ran while one was open for 47% of the time, Pallas kernels for 0%

commit v1 on v0

--- a/solution.py
+++ b/solution.py
@@ -1,13 +1,312 @@
+import functools
 import math
 
 import jax
 import jax.numpy as jnp
 import numpy as np
 from jax import lax
+from jax.experimental import pallas as pl
+from jax.experimental.pallas import tpu as pltpu
 from jax.sharding import PartitionSpec as P
 
 HD = 128
-CH = 4096
+LANES = 128
+MESH = pl.DeviceIdType.MESH
+
+
+def fused_kernel(
+    n,
+    n_grp,
+    streams,
+    filters,
+    gain,
+    out,
+    buf,
+    taps,
+    toep,
+    feat,
+    scores,
+    top,
+    total,
+    accum,
+    sending,
+    att,
+    sums,
+    local_sem,
+    send_sem,
+    recv_sem,
+    back_send,
+    back_recv,
+    sum_send,
+    sum_recv,
+):
+    me = lax.axis_index("ctx")
+    my_grp = lax.axis_index("grp")
+    rows = streams.shape[1]
+    chans = streams.shape[2]
+    groups = filters.shape[1]
+    flen = filters.shape[2]
+    cols = chans // n
+    width = chans // groups
+    own_groups = groups // n
+    per_tile = LANES // width
+    heads = cols // HD
+
+    def col_of(j):
+        return pl.ds(pl.multiple_of(j * cols, cols), cols)
+
+    def row_of(i):
+        return pl.ds(pl.multiple_of(flen + i * rows, flen), rows)
+
+    barrier = pltpu.get_barrier_semaphore()
+    for k in range(1, n):
+        pl.semaphore_signal(
+            barrier, inc=1, device_id={"ctx": lax.rem(me + k, n)}, device_id_type=MESH
+        )
+    for k in range(1, n_grp):
+        pl.semaphore_signal(
+            barrier, inc=1, device_id={"grp": lax.rem(my_grp + k, n_grp)}, device_id_type=MESH
+        )
+    pl.semaphore_wait(barrier, n - 1 + n_grp - 1)
+
+    def stream_copy(s, target, source):
+        return pltpu.make_async_remote_copy(
+            src_ref=streams.at[s, :, col_of(target)],
+            dst_ref=buf.at[s, row_of(source), :],
+            send_sem=send_sem.at[target, s],
+            recv_sem=recv_sem.at[source, s],
+            device_id={"ctx": target},
+            device_id_type=MESH,
+        )
+
+    def own_copy(s):
+        return pltpu.make_async_copy(
+            streams.at[s, :, col_of(me)], buf.at[s, row_of(me), :], local_sem.at[s]
+        )
+
+    for k in range(1, n):
+        target = lax.rem(me + k, n)
+        for s in range(3):
+            stream_copy(s, target, me).start()
+    for s in range(3):
+        own_copy(s).start()
+
+    for s in range(3):
+        buf[s, pl.ds(0, flen), :] = jnp.zeros((flen, cols), buf.dtype)
+    taps[...] = filters[...].astype(jnp.float32)
+    row_id = lax.broadcasted_iota(jnp.int32, (flen, flen), 0)
+    col_id = lax.broadcasted_iota(jnp.int32, (flen, flen), 1)
+
+    @pl.loop(0, 3 * own_groups)
+    def _(idx):
+        s = idx // own_groups
+        g = lax.rem(idx, own_groups)
+        line = taps[s, pl.ds(me * own_groups + g, 1), :]
+        turned = pltpu.roll(
+            jnp.broadcast_to(line, (flen, flen)), 0, 1, stride=1, stride_axis=0
+        ).T
+        lower = jnp.where(col_id <= row_id, turned, 0.0)
+        upper = jnp.where(col_id > row_id, turned, 0.0)
+        where = pl.ds(pl.multiple_of(g * flen, flen), flen)
+        toep[s, where, pl.ds(0, flen)] = upper.astype(toep.dtype)
+        toep[s, where, pl.ds(flen, flen)] = lower.astype(toep.dtype)
+
+    blocks = rows // flen
+    lane_group = lax.broadcasted_iota(jnp.int32, (flen, blocks * LANES), 1)
+    lane_group = lax.rem(lane_group, LANES) // width
+    factor = HD ** (-0.5) * math.log2(math.e)
+
+    def fold(values, op):
+        result = values[:, :LANES]
+        for c in range(1, values.shape[1] // LANES):
+            result = op(result, values[:, c * LANES : (c + 1) * LANES])
+        return result
+
+    def filter_block(i):
+        @pl.loop(0, 3)
+        def _(s):
+            for h in range(heads):
+                lanes = pl.ds(h * LANES, LANES)
+                window = [
+                    buf[s, pl.ds(pl.multiple_of(i * rows + b * flen, flen), 2 * flen), lanes]
+                    for b in range(blocks)
+                ]
+                matrix = toep[s, pl.ds(h * per_tile * flen, per_tile * flen), :]
+                product = jnp.dot(
+                    matrix, jnp.concatenate(window, axis=1), preferred_element_type=jnp.float32
+                )
+                result = product[:flen]
+                for g in range(1, per_tile):
+                    result = jnp.where(
+                        lane_group == g, product[g * flen : (g + 1) * flen], result
+                    )
+                result = result.astype(feat.dtype)
+                for b in range(blocks):
+                    feat[
+                        s, pl.ds(pl.multiple_of(i * rows + b * flen, flen), flen), lanes
+                    ] = result[:, b * LANES : (b + 1) * LANES]
+
+    def rows_at(j):
+        return pl.ds(pl.multiple_of(j * rows, flen), rows)
+
+    def attend_block(i, h):
+        lanes = pl.ds(h * HD, HD)
+        query = feat[0, rows_at(i), lanes]
+
+        def score(j):
+            return lax.dot_general(
+                query,
+                feat[1, rows_at(j), lanes],
+                (((1,), (1,)), ((), ())),
+                preferred_element_type=jnp.float32,
+            )
+
+        place = lax.broadcasted_iota(jnp.int32, (rows, rows), 0)
+        other = lax.broadcasted_iota(jnp.int32, (rows, rows), 1)
+        diagonal = jnp.where(other <= place, score(i), -1e30)
+        scores[i] = diagonal
+        top[...] = fold(diagonal, jnp.maximum)
+
+        @pl.loop(0, i)
+        def _(j):
+            block = score(j)
+            scores[j] = block
+            top[...] = jnp.maximum(top[...], fold(block, jnp.maximum))
+
+        highest = jnp.max(top[...], axis=1, keepdims=True)
+        top[...] = jnp.broadcast_to(highest, top.shape)
+        total[...] = jnp.zeros_like(total)
+        accum[...] = jnp.zeros_like(accum)
+
+        @pl.loop(0, i + 1)
+        def _(j):
+            weights = jnp.exp2((scores[j] - top[:, :1]) * factor)
+            total[...] += fold(weights, jnp.add)
+            accum[...] += jnp.dot(
+                weights.astype(jnp.bfloat16),
+                feat[2, rows_at(j), lanes],
+                preferred_element_type=jnp.float32,
+            )
+
+        sum_of = jnp.sum(total[...], axis=1, keepdims=True)
+        return (accum[...] / sum_of).astype(jnp.bfloat16)
+
+    def back_copy(target, source):
+        return pltpu.make_async_remote_copy(
+            src_ref=sending.at[target],
+            dst_ref=att.at[:, col_of(source)],
+            send_sem=back_send.at[target],
+            recv_sem=back_recv.at[source],
+            device_id={"ctx": target},
+            device_id_type=MESH,
+        )
+
+    @pl.loop(0, n)
+    def _(i):
+        @pl.when(i != me)
+        def _():
+            for s in range(3):
+                stream_copy(s, i, i).wait_recv()
+
+        @pl.when(i == me)
+        def _():
+            for s in range(3):
+                own_copy(s).wait()
+
+        filter_block(i)
+        for h in range(heads):
+            sending[i, :, pl.ds(h * HD, HD)] = attend_block(i, h)
+
+        @pl.when(i != me)
+        def _():
+            back_copy(i, me).start()
+
+        @pl.when(i == me)
+        def _():
+            att[:, col_of(me)] = sending[i]
+
+    for k in range(1, n):
+        source = lax.rem(me + k, n)
+        back_copy(source, source).wait_recv()
+
+    @pl.loop(0, blocks)
+    def _(b):
+        part = pl.ds(pl.multiple_of(b * flen, flen), flen)
+        wide = att[part, :].astype(jnp.float32)
+        squares = fold(wide * wide, jnp.add).T
+        squares = squares.reshape(LANES // 8, 8, flen)
+        sums[0, :, part] = jnp.sum(squares, axis=0)
+
+    def sum_copy(k, turn):
+        return pltpu.make_async_remote_copy(
+            src_ref=sums.at[0],
+            dst_ref=sums.at[k],
+            send_sem=sum_send.at[k],
+            recv_sem=sum_recv.at[k],
+            device_id={"grp": lax.rem(my_grp + turn, n_grp)},
+            device_id_type=MESH,
+        )
+
+    for k in range(1, n_grp):
+        sum_copy(k, k).start()
+    for k in range(1, n_grp):
+        sum_copy(k, k).wait()
+
+    @pl.loop(0, blocks)
+    def _(b):
+        part = pl.ds(pl.multiple_of(b * flen, flen), flen)
+        power = sums[0, :, part]
+        for k in range(1, n_grp):
+            power = power + sums[k, :, part]
+        power = jnp.sum(power, axis=0, keepdims=True) / (chans * n_grp)
+        power = jnp.broadcast_to(lax.rsqrt(power + 1e-06), (LANES, flen)).T
+        wide = att[part, :].astype(jnp.float32)
+        for c in range(chans // LANES):
+            lanes = slice(c * LANES, (c + 1) * LANES)
+            out[part, lanes] = (wide[:, lanes] * gain[:, lanes] * power).astype(out.dtype)
+
+    for k in range(1, n):
+        target = lax.rem(me + k, n)
+        for s in range(3):
+            stream_copy(s, target, me).wait_send()
+        back_copy(target, me).wait_send()
+
+
+def fused(streams, filters, gain):
+    n, n_grp = lax.axis_size("ctx"), lax.axis_size("grp")
+    _, rows, chans = streams.shape
+    _, groups, flen = filters.shape
+    cols = chans // n
+    tokens = rows * n
+    vmem = pl.BlockSpec(memory_space=pltpu.VMEM)
+    return pl.pallas_call(
+        functools.partial(fused_kernel, n, n_grp),
+        out_shape=jax.ShapeDtypeStruct((rows, chans), jnp.bfloat16),
+        in_specs=[pl.BlockSpec(memory_space=pl.ANY), vmem, vmem],
+        out_specs=vmem,
+        scratch_shapes=[
+            pltpu.VMEM((3, flen + tokens, cols), jnp.bfloat16),
+            pltpu.VMEM((3, groups, flen), jnp.float32),
+            pltpu.VMEM((3, groups // n * flen, 2 * flen), jnp.bfloat16),
+            pltpu.VMEM((3, tokens, cols), jnp.bfloat16),
+            pltpu.VMEM((n, rows, rows), jnp.float32),
+            pltpu.VMEM((rows, LANES), jnp.float32),
+            pltpu.VMEM((rows, LANES), jnp.float32),
+            pltpu.VMEM((rows, HD), jnp.float32),
+            pltpu.VMEM((n, rows, cols), jnp.bfloat16),
+            pltpu.VMEM((rows, chans), jnp.bfloat16),
+            pltpu.VMEM((n_grp, 8, rows), jnp.float32),
+            pltpu.SemaphoreType.DMA((3,)),
+            pltpu.SemaphoreType.DMA((n, 3)),
+            pltpu.SemaphoreType.DMA((n, 3)),
+            pltpu.SemaphoreType.DMA((n,)),
+            pltpu.SemaphoreType.DMA((n,)),
+            pltpu.SemaphoreType.DMA((n_grp,)),
+            pltpu.SemaphoreType.DMA((n_grp,)),
+        ],
+        compiler_params=pltpu.CompilerParams(collective_id=0, has_side_effects=True),
+        name="fused",
+    )(streams, filters, gain.reshape(1, chans))
 
 
 def passed_along(block, axis, distance):
@@ -102,12 +401,23 @@
     positions = my_index * tok_rows + jnp.arange(tok_rows, dtype=jnp.int32)
     attended = attend(queries, positions, features[1], features[2])
     wide = attended.astype(jnp.float32)
-    power = lax.psum(jnp.sum(wide * wide, axis=1), "grp") / CH
+    power = lax.psum(jnp.sum(wide * wide, axis=1), "grp") / (streams.shape[2] * lax.axis_size("grp"))
     return (wide * gain[None, :] * lax.rsqrt(power + 1e-06)[:, None]).astype(jnp.bfloat16)
+
+
+def chosen(streams, filters, gain):
+    n = lax.axis_size("ctx")
+    _, rows, chans = streams.shape
+    _, groups, flen = filters.shape
+    whole_heads = chans % (n * HD) == 0
+    fits = flen == LANES and rows % flen == 0 and LANES % (chans // groups) == 0
+    if n > 1 and whole_heads and fits and groups % n == 0:
+        return fused(streams, filters, gain)
+    return local(streams, filters, gain)
 
 
 def solution(mesh):
     placed = (P(None, "ctx", "grp"), P(None, "grp", None), P("grp"))
     return jax.shard_map(
-        local, mesh=mesh, in_specs=placed, out_specs=P("ctx", "grp"), check_vma=False
+        chosen, mesh=mesh, in_specs=placed, out_specs=P("ctx", "grp"), check_vma=False
     )

time: 570 us -> 102 us (0.18)
  local copies, waits for them, and re-layouts: 294 us -> 2.06 us
  waiting for transfers between devices: 195 us -> 0 us
  Pallas kernels: 0 us -> 100 us
  matrix products: 37.7 us -> 0 us
  other arithmetic: 14.4 us -> 0 us
  between operations: 13.6 us -> 0.01 us
    gather x4 -> x0, local copies, waits for them, and re-layouts: 260 us -> none  [the longest x2 130 us: filter_all(): upper = jnp.where(lag_table < 0, filters[:, :, upper_idx], 0.0)]
    all_gather x2 -> x0, waiting for transfers between devices: 195 us -> none  [the longest x1 99.8 us: attend(): value_piece = lax.all_gather(valued, 'ctx', axis=0, tiled=True)]
    pallas_call x0 -> x1, Pallas kernels: none -> 100 us  [fused(): pl.pallas_call(functools.partial(fused_kernel, n, n_grp), out_shape=jax.S...]
    dot_general x14 -> x0, matrix products: 37.7 us -> none  [the longest x6 14.9 us: update_block(): jnp.einsum('hsk,khd->shd', weights.astype(jnp.bfloat16), value_block, pre...]
    slice x6 -> x0, local copies, waits for them, and re-layouts: 11.2 us -> none  [the longest x1 8.05 us: filter_all(): blocks[:, 1:]]
    dynamic_slice x6 -> x0, local copies, waits for them, and re-layouts: 10.1 us -> none  [step_block(): lax.dynamic_slice_in_dim(value_piece, offset, block_len, 0)]
    reduce_sum x7 -> x0, other arithmetic: 8.44 us -> none  [the longest x6 7.87 us: update_block(): totals = totals * factor + jnp.sum(weights, axis=2)]
  transfers between devices with their start and end apart: 3 -> 0, of which waited for: 2 -> 0; matrix products, arithmetic and copies ran while one was open for 47% -> 0% of each run, Pallas kernels for 0% -> 0%
where the time goes in v1:
time: 102 us
  Pallas kernels  100 us (98%)
  local copies, waits for them, and re-layouts  2.06 us (2%)
    pallas_call x1, Pallas kernels, fused(): pl.pallas_call(functools.partial(fused_kernel, n, n_grp), out_shape=jax.S...  100 us
    unnamed x1, local copies, waits for them, and re-layouts  2.06 us

profile of v1, /device:TPU:29, one launch (start us, length us, event | category | flops | bytes accessed | tf_op | source)
XLA Modules:
  0.0 102.1 jit_solution(8240495735770515329)
XLA Ops:
  0.0 100.0 %fused.1 = bf16[384,1024]{1,0:T(8,128)(2,1)} custom-call(bf16[3,384,1024]{2,1,0:T(8,128)(2,1)} %streams.1, bf16[3,64,128]{2,1,0:T(8,128)(2,1)} %filters.1, f32[1,1024]{1,0:T(1,128)} %bitcast.1), custom_call_target="tpu_custom_call" | custom-call | tf_op jit(solution)/shard_map/fused/pallas_call | solution.py:282
  100.0 2.1 %copy.5 = bf16[384,1024]{1,0:T(8,128)(2,1)} copy(bf16[384,1024]{1,0:T(8,128)(2,1)} %fused.1) | data formatting | bytes 1572864

commit v2 on v1

--- a/solution.py
+++ b/solution.py
@@ -25,7 +25,6 @@
     taps,
     toep,
     feat,
-    scores,
     top,
     total,
     accum,
@@ -69,27 +68,35 @@
         )
     pl.semaphore_wait(barrier, n - 1 + n_grp - 1)
 
-    def stream_copy(s, target, source):
+    def target_at(k):
+        return jnp.bitwise_xor(me, k) if n & (n - 1) == 0 else lax.rem(me + k, n)
+
+    def source_at(k):
+        return jnp.bitwise_xor(me, k) if n & (n - 1) == 0 else lax.rem(me - k + n, n)
+
+    spans = ((rows - flen, flen), (0, rows - flen))
+
+    def stream_copy(p, target, source):
+        first, size = spans[p]
+        start = pl.multiple_of(flen + source * rows + first, flen)
         return pltpu.make_async_remote_copy(
-            src_ref=streams.at[s, :, col_of(target)],
-            dst_ref=buf.at[s, row_of(source), :],
-            send_sem=send_sem.at[target, s],
-            recv_sem=recv_sem.at[source, s],
+            src_ref=streams.at[:, pl.ds(first, size), col_of(target)],
+            dst_ref=buf.at[:, pl.ds(start, size), :],
+            send_sem=send_sem.at[target, p],
+            recv_sem=recv_sem.at[source, p],
             device_id={"ctx": target},
             device_id_type=MESH,
         )
 
-    def own_copy(s):
+    def own_copy():
         return pltpu.make_async_copy(
-            streams.at[s, :, col_of(me)], buf.at[s, row_of(me), :], local_sem.at[s]
-        )
-
-    for k in range(1, n):
-        target = lax.rem(me + k, n)
-        for s in range(3):
-            stream_copy(s, target, me).start()
-    for s in range(3):
-        own_copy(s).start()
+            streams.at[:, :, col_of(me)], buf.at[:, row_of(me), :], local_sem.at[0]
+        )
+
+    own_copy().start()
+    for p in range(2):
+        for k in range(1, n):
+            stream_copy(p, target_at(k), me).start()
 
     for s in range(3):
         buf[s, pl.ds(0, flen), :] = jnp.zeros((flen, cols), buf.dtype)
@@ -149,47 +156,48 @@
     def rows_at(j):
         return pl.ds(pl.multiple_of(j * rows, flen), rows)
 
-    def attend_block(i, h):
+    def score(q, key, h):
         lanes = pl.ds(h * HD, HD)
-        query = feat[0, rows_at(i), lanes]
-
-        def score(j):
-            return lax.dot_general(
-                query,
-                feat[1, rows_at(j), lanes],
-                (((1,), (1,)), ((), ())),
-                preferred_element_type=jnp.float32,
-            )
-
+        return lax.dot_general(
+            feat[0, rows_at(q), lanes],
+            feat[1, rows_at(key), lanes],
+            (((1,), (1,)), ((), ())),
+            preferred_element_type=jnp.float32,
+        )
+
+    def mixed(weights, key, h):
+        return jnp.dot(
+            weights.astype(jnp.bfloat16),
+            feat[2, rows_at(key), pl.ds(h * HD, HD)],
+            preferred_element_type=jnp.float32,
+        )
+
+    def open_block(q, h):
         place = lax.broadcasted_iota(jnp.int32, (rows, rows), 0)
         other = lax.broadcasted_iota(jnp.int32, (rows, rows), 1)
-        diagonal = jnp.where(other <= place, score(i), -1e30)
-        scores[i] = diagonal
-        top[...] = fold(diagonal, jnp.maximum)
-
-        @pl.loop(0, i)
-        def _(j):
-            block = score(j)
-            scores[j] = block
-            top[...] = jnp.maximum(top[...], fold(block, jnp.maximum))
-
-        highest = jnp.max(top[...], axis=1, keepdims=True)
-        top[...] = jnp.broadcast_to(highest, top.shape)
-        total[...] = jnp.zeros_like(total)
-        accum[...] = jnp.zeros_like(accum)
-
-        @pl.loop(0, i + 1)
-        def _(j):
-            weights = jnp.exp2((scores[j] - top[:, :1]) * factor)
-            total[...] += fold(weights, jnp.add)
-            accum[...] += jnp.dot(
-                weights.astype(jnp.bfloat16),
-                feat[2, rows_at(j), lanes],
-                preferred_element_type=jnp.float32,
-            )
-
-        sum_of = jnp.sum(total[...], axis=1, keepdims=True)
-        return (accum[...] / sum_of).astype(jnp.bfloat16)
+        block = jnp.where(other <= place, score(q, q, h), -1e30)
+        new = jnp.max(fold(block, jnp.maximum), axis=1, keepdims=True)
+        weights = jnp.exp2((block - new) * factor)
+        at = q * heads + h
+        top[at] = jnp.broadcast_to(new, (rows, LANES))
+        total[at] = fold(weights, jnp.add)
+        accum[at] = mixed(weights, q, h)
+
+    def add_block(q, key, h):
+        at = q * heads + h
+        block = score(q, key, h)
+        old = top[at]
+        new = jnp.maximum(old, jnp.max(fold(block, jnp.maximum), axis=1, keepdims=True))
+        shrink = jnp.exp2((old - new) * factor)
+        weights = jnp.exp2((block - new[:, :1]) * factor)
+        top[at] = new
+        total[at] = total[at] * shrink + fold(weights, jnp.add)
+        accum[at] = accum[at] * shrink + mixed(weights, key, h)
+
+    def close_block(q, h):
+        at = q * heads + h
+        sum_of = jnp.sum(total[at], axis=1, keepdims=True)
+        return (accum[at] / sum_of).astype(jnp.bfloat16)
 
     def back_copy(target, source):
         return pltpu.make_async_remote_copy(
@@ -201,21 +209,33 @@
             device_id_type=MESH,
         )
 
+    for k in range(1, n):
+        source = source_at(k)
+        stream_copy(0, source, source).wait_recv()
+    own_copy().wait()
+
     @pl.loop(0, n)
-    def _(i):
-        @pl.when(i != me)
+    def _(k):
+        b = source_at(k)
+
+        @pl.when(k > 0)
         def _():
-            for s in range(3):
-                stream_copy(s, i, i).wait_recv()
-
-        @pl.when(i == me)
-        def _():
-            for s in range(3):
-                own_copy(s).wait()
-
-        filter_block(i)
+            stream_copy(1, b, b).wait_recv()
+
+        filter_block(b)
         for h in range(heads):
-            sending[i, :, pl.ds(h * HD, HD)] = attend_block(i, h)
+            open_block(b, h)
+
+            @pl.loop(0, k)
+            def _(before):
+                o = source_at(before)
+                add_block(jnp.maximum(b, o), jnp.minimum(b, o), h)
+
+    @pl.loop(0, n)
+    def _(k):
+        i = source_at(n - 1 - k)
+        for h in range(heads):
+            sending[i, :, pl.ds(h * HD, HD)] = close_block(i, h)
 
         @pl.when(i != me)
         def _():
@@ -267,8 +287,8 @@
 
     for k in range(1, n):
         target = lax.rem(me + k, n)
-        for s in range(3):
-            stream_copy(s, target, me).wait_send()
+        for p in range(2):
+            stream_copy(p, target, me).wait_send()
         back_copy(target, me).wait_send()
 
 
@@ -289,16 +309,15 @@
             pltpu.VMEM((3, groups, flen), jnp.float32),
             pltpu.VMEM((3, groups // n * flen, 2 * flen), jnp.bfloat16),
             pltpu.VMEM((3, tokens, cols), jnp.bfloat16),
-            pltpu.VMEM((n, rows, rows), jnp.float32),
-            pltpu.VMEM((rows, LANES), jnp.float32),
-            pltpu.VMEM((rows, LANES), jnp.float32),
-            pltpu.VMEM((rows, HD), jnp.float32),
+            pltpu.VMEM((chans // HD, rows, LANES), jnp.float32),
+            pltpu.VMEM((chans // HD, rows, LANES), jnp.float32),
+            pltpu.VMEM((chans // HD, rows, HD), jnp.float32),
             pltpu.VMEM((n, rows, cols), jnp.bfloat16),
             pltpu.VMEM((rows, chans), jnp.bfloat16),
             pltpu.VMEM((n_grp, 8, rows), jnp.float32),
-            pltpu.SemaphoreType.DMA((3,)),
-            pltpu.SemaphoreType.DMA((n, 3)),
-            pltpu.SemaphoreType.DMA((n, 3)),
+            pltpu.SemaphoreType.DMA((1,)),
+            pltpu.SemaphoreType.DMA((n, 2)),
+            pltpu.SemaphoreType.DMA((n, 2)),
             pltpu.SemaphoreType.DMA((n,)),
             pltpu.SemaphoreType.DMA((n,)),
             pltpu.SemaphoreType.DMA((n_grp,)),

time: 102 us -> 93.5 us (0.917)
  the two profiles are of different devices: /device:TPU:29 before, /device:TPU:0 now
where the time goes in v2:
time: 93.5 us; the launch traced here: 93.3 us
  Pallas kernels  91.2 us (98%)
  local copies, waits for them, and re-layouts  2.06 us (2%)
    pallas_call x1, Pallas kernels, fused(): pl.pallas_call(functools.partial(fused_kernel, n, n_grp), out_shape=jax.S...  91.2 us
    unnamed x1, local copies, waits for them, and re-layouts  2.06 us

profile of v2, /device:TPU:0, one launch (start us, length us, event | category | flops | bytes accessed | tf_op | source)
XLA Modules:
  0.0 93.3 jit_solution(16962551992719332753)
XLA Ops:
  0.0 91.2 %fused.1 = bf16[384,1024]{1,0:T(8,128)(2,1)} custom-call(bf16[3,384,1024]{2,1,0:T(8,128)(2,1)} %streams.1, bf16[3,64,128]{2,1,0:T(8,128)(2,1)} %filters.1, f32[1,1024]{1,0:T(1,128)} %bitcast.1), custom_call_target="tpu_custom_call" | custom-call | tf_op jit(solution)/shard_map/fused/pallas_call | solution.py:302
  91.2 2.1 %copy.5 = bf16[384,1024]{1,0:T(8,128)(2,1)} copy(bf16[384,1024]{1,0:T(8,128)(2,1)} %fused.1) | data formatting | bytes 1572864
